TPU v7x, 32 devices: a whole 2x2x4 slice. The times are simulated.
32 devices in a mesh: cfg: 2 (over core), seq: 8 (over z, y), mlp: 2 (over x).
Axes of the slice: x: 2, y: 2, z: 4, core: 2. Of those that a mesh axis runs over, the one named last changes fastest.
Arguments:
- image_hidden: bfloat16 [2, 256, 8, 1536], P('cfg', ('seq', 'mlp')), may hold values from -6 to 6
- text_hidden: bfloat16 [2, 1232, 1536], P('cfg', 'seq'), may hold values from -6 to 6
- modulation: float32 [2, 8, 10, 1536], P('cfg'), may hold values from -3 to 3
- text_lengths: int32 [2, 8], P('cfg'), may hold values from 1 to 154, as said below
- timestep: int32 [1], replicated, may hold values from 0 to 27
- latent: float32 [256, 8, 64], P(('seq', 'mlp'), 'cfg'), may hold values from -6 to 6
- w_qkv: bfloat16 [3, 1536, 1536], P(None, None, 'mlp'), may hold values from -0.15625 to 0.15625
- w_out: bfloat16 [1536, 1536], P('mlp'), may hold values from -0.15625 to 0.15625
- w_text_kv: bfloat16 [2, 1536, 1536], P(None, None, 'mlp'), may hold values from -0.15625 to 0.15625
- norm_gain: float32 [3, 64], replicated, may hold values from 1 to 2
- w_up: bfloat16 [1536, 6144], P(None, 'mlp'), may hold values from -0.15625 to 0.15625
- w_down: bfloat16 [6144, 1536], P('mlp'), may hold values from -0.078125 to 0.078125
- w_head: bfloat16 [1536, 64], replicated, may hold values from -0.078125 to 0.078125
Outputs:
- velocity: float32 [256, 8, 64], P(('seq', 'mlp'), 'cfg')
- next_latent: float32 [256, 8, 64], P(('seq', 'mlp'), 'cfg')
- denoised: float32 [256, 8, 64], P(('seq', 'mlp'), 'cfg')
Inputs may be any that keep to these rules, and one draw needn't show every extreme that they name: Text position j of prompt b in half c is a real token only if j < text_lengths[c, b]; in every draw some length equals 154 and some equals 1.
All inputs are finite; a program needn't handle non-finite values.
Results may differ from a plain program's by a relative error of at most 0.0085.
Values may be sent and summed in bfloat16 or wider, within the bound.
A program may use at most 128 MiB of HBM per device.

v0:
```python
import math
import jax
import jax.numpy as jnp
from jax import lax
from jax.sharding import PartitionSpec as P

HEAD_DIM = 64
TXT = 154
STEPS = 28
EPS = 1e-06
GUIDE = 4.5
SHIFT = 3.0


def partner_2(block, axis, stride):
    count = lax.axis_size(axis)
    route = []
    for low in range(count):
        high = low | 1 << stride
        if high != low and high < count:
            route += [(low, high), (high, low)]
    return lax.ppermute(block, axis, route)


def layer_norm(values):
    mean = jnp.mean(values, axis=-1, keepdims=True)
    centred = values - mean
    spread = jnp.mean(centred * centred, axis=-1, keepdims=True)
    return centred * lax.rsqrt(spread + EPS)


def modulate(values, shift, scale):
    return layer_norm(values) * (1.0 + scale) + shift


def head_norm(values, gain):
    shaped = values.reshape(values.shape[:-1] + (values.shape[-1] // HEAD_DIM, HEAD_DIM))
    square = jnp.mean(shaped * shaped, axis=-1, keepdims=True)
    return (shaped * lax.rsqrt(square + EPS) * gain).astype(jnp.bfloat16)


def sigma_of(index):
    level = 1.0 - index.astype(jnp.float32) / STEPS
    return SHIFT * level / (1.0 + (SHIFT - 1.0) * level)


def project_image(normed_rows, w_qkv, norm_gain):
    query = head_norm(
        jnp.einsum("tbd,de->tbe", normed_rows, w_qkv[0], preferred_element_type=jnp.float32),
        norm_gain[0],
    )
    keys = head_norm(
        jnp.einsum("tbd,de->tbe", normed_rows, w_qkv[1], preferred_element_type=jnp.float32),
        norm_gain[1],
    )
    values = jnp.einsum(
        "tbd,de->tbe", normed_rows, w_qkv[2], preferred_element_type=jnp.float32
    ).astype(jnp.bfloat16)
    flat_query = query.reshape(query.shape[:-2] + (-1,))
    flat_keys = keys.reshape(keys.shape[:-2] + (-1,))
    return jnp.concatenate([flat_query, flat_keys, values], axis=-1)


def key_terms(query, key_rows, value_rows, keep):
    factor = 1.0 / math.sqrt(HEAD_DIM)
    prompts = query.shape[1]
    if keep is None:
        keep = jnp.ones((prompts, key_rows.shape[0]), jnp.float32)

    def one_prompt(items):
        query_rows, keys_one, values_one, keep_one = items
        scores = (
            jnp.einsum("qhd,khd->hqk", query_rows, keys_one, preferred_element_type=jnp.float32)
            * factor
        )
        weights = jnp.exp(scores) * keep_one[None, None, :]
        numer = jnp.einsum(
            "hqk,khd->hqd",
            weights.astype(jnp.bfloat16),
            values_one,
            preferred_element_type=jnp.float32,
        )
        return (numer, jnp.sum(weights, axis=-1))

    return lax.map(
        one_prompt,
        (
            jnp.moveaxis(query, 1, 0),
            jnp.moveaxis(key_rows, 1, 0),
            jnp.moveaxis(value_rows, 1, 0),
            keep,
        ),
    )


def shards(
    image_hidden,
    text_hidden,
    modulation,
    text_lengths,
    timestep,
    latent,
    w_qkv,
    w_out,
    w_text_kv,
    norm_gain,
    w_up,
    w_down,
    w_head,
):
    mods = modulation[0]
    own_hidden = image_hidden[0]
    rows = own_hidden.shape[0]
    width = w_out.shape[0]
    heads = width // HEAD_DIM
    prompts = mods.shape[0]
    offset = lax.axis_index("mlp") * rows
    block_hidden = lax.all_gather(own_hidden, "mlp", axis=0, tiled=True).astype(jnp.float32)
    normed = modulate(block_hidden, mods[:, 0], mods[:, 1]).astype(jnp.bfloat16)
    projected = project_image(normed, w_qkv, norm_gain)
    block_rows = projected.shape[0]
    query = projected[..., :width].reshape(block_rows, prompts, heads, HEAD_DIM)
    own_pairs = projected[..., width:]
    text_rows = text_hidden.shape[1]
    position = lax.axis_index("seq") * text_rows + lax.iota(jnp.int32, text_rows)
    owner = position // TXT
    pick = (owner[:, None] == lax.iota(jnp.int32, prompts)[None, :]).astype(jnp.float32)
    text_shift = jnp.dot(pick, mods[:, 6], precision=lax.Precision.HIGHEST)
    text_scale = jnp.dot(pick, mods[:, 7], precision=lax.Precision.HIGHEST)
    text_normed = modulate(text_hidden[0].astype(jnp.float32), text_shift, text_scale).astype(
        jnp.bfloat16
    )
    text_keys = head_norm(
        jnp.dot(text_normed, w_text_kv[0], preferred_element_type=jnp.float32), norm_gain[2]
    )
    text_keys = text_keys.reshape(text_rows, width)
    text_values = jnp.dot(text_normed, w_text_kv[1], preferred_element_type=jnp.float32).astype(
        jnp.bfloat16
    )
    text_pairs = jnp.concatenate([text_keys, text_values], axis=-1)
    keep = (lax.iota(jnp.int32, TXT)[None, :] < text_lengths[0][:, None]).astype(jnp.float32)

    def split_pairs(pairs):
        shape = pairs.shape[:2] + (heads, HEAD_DIM)
        return (pairs[..., :width].reshape(shape), pairs[..., width:].reshape(shape))

    all_image, all_text = (
        lax.all_gather(own_pairs, "seq", axis=0, tiled=True),
        lax.all_gather(text_pairs, "seq", axis=0, tiled=True),
    )
    shaped = jnp.transpose(all_text.reshape(prompts, TXT, 2 * width), (1, 0, 2))
    key_rows, value_rows = split_pairs(shaped)
    text_numer, text_denom = key_terms(query, key_rows, value_rows, keep)
    key_rows, value_rows = split_pairs(all_image)
    image_numer, image_denom = key_terms(query, key_rows, value_rows, None)
    numer = text_numer + image_numer
    denom = text_denom + image_denom
    attended = (numer / denom[..., None]).astype(jnp.bfloat16)
    attended = jnp.transpose(attended, (2, 0, 1, 3)).reshape(block_rows, prompts, width)
    part = attended
    attention_out = lax.psum(
        jnp.einsum("tbe,ed->tbd", part, w_out, preferred_element_type=jnp.float32).astype(
            jnp.bfloat16
        ),
        "mlp",
    ).astype(jnp.float32)
    first = block_hidden + mods[:, 2] * attention_out
    mlp_in = modulate(first, mods[:, 3], mods[:, 4]).astype(jnp.bfloat16)
    raised = jnp.einsum("tbd,du->tbu", mlp_in, w_up, preferred_element_type=jnp.float32)
    activated = jax.nn.gelu(raised, approximate=True).astype(jnp.bfloat16)
    own_first = lax.dynamic_slice_in_dim(first, offset, rows, 0)
    part = activated
    mlp_out = lax.psum_scatter(
        jnp.einsum("tbu,ud->tbd", part, w_down, preferred_element_type=jnp.float32).astype(
            jnp.bfloat16
        ),
        "mlp",
        scatter_dimension=0,
        tiled=True,
    ).astype(jnp.float32)
    second = own_first + mods[:, 5] * mlp_out
    final = modulate(second, mods[:, 8], mods[:, 9]).astype(jnp.bfloat16)
    own_velocity = jnp.einsum("tbd,dp->tbp", final, w_head, preferred_element_type=jnp.float32)
    half_count = prompts // 2
    branch = lax.axis_index("cfg")
    outgoing = lax.dynamic_slice_in_dim(own_velocity, (1 - branch) * half_count, half_count, 1)
    kept = lax.dynamic_slice_in_dim(own_velocity, branch * half_count, half_count, 1)
    partner = partner_2(outgoing, "cfg", 0)
    is_conditional = branch == 0
    conditional = jnp.where(is_conditional, kept, partner)
    unconditional = jnp.where(is_conditional, partner, kept)
    velocity = unconditional + GUIDE * (conditional - unconditional)
    sigma_now = sigma_of(timestep[0])
    sigma_after = sigma_of(timestep[0] + 1)
    next_latent = latent + (sigma_after - sigma_now) * velocity
    denoised = latent - sigma_now * velocity
    return (velocity, next_latent, denoised)


def solution(mesh):
    placed = (
        P("cfg", ("seq", "mlp"), None, None),
        P("cfg", "seq", None),
        P("cfg", None, None, None),
        P("cfg", None),
        P(),
        P(("seq", "mlp"), "cfg", None),
        P(None, None, "mlp"),
        P("mlp", None),
        P(None, None, "mlp"),
        P(),
        P(None, "mlp"),
        P("mlp", None),
        P(),
    )
    return jax.shard_map(
        shards,
        mesh=mesh,
        in_specs=placed,
        out_specs=(
            P(("seq", "mlp"), "cfg", None),
            P(("seq", "mlp"), "cfg", None),
            P(("seq", "mlp"), "cfg", None),
        ),
        check_vma=False,
    )
```

profile of v0, /device:TPU:0, one launch (start us, length us, event | category | flops | bytes accessed | tf_op | source)
XLA Modules:
  0.0 328.8 jit_solution(14662058543458932708)
XLA Ops:
  14.3 3.2 slice_bitcast_fusion.1
  17.5 4.3 %copy.71 = bf16[768,1536]{1,0:T(8,128)(2,1)} copy(bf16[768,1536]{0,1:T(8,128)(2,1)} %slice_bitcast_fusion.1) | data formatting | bytes 4718592 | tf_op jit(solution)/shard_map/dot_general | solution.py:134
  21.8 2.4 fusion.64
  26.2 4.8 %slice_bitcast_fusion = (bf16[768,1536]{0,1:T(8,128)(2,1)}, bf16[768,1536]{0,1:T(8,128)(2,1)}) fusion(bf16[3,1536,768]{2,1,0:T(8,128)(2,1)} %param.23), kind=kLoop, calls=%fused_computation.55 | loop fusion | bytes 9437184 | tf_op jit(solution)/shard_map/tbd,de->tbe/dot_general | solution.py:53
  31.1 4.4 %copy.75 = bf16[768,1536]{1,0:T(8,128)(2,1)} copy(bf16[768,1536]{0,1:T(8,128)(2,1)} %get-tuple-element.177) | data formatting | bytes 4718592 | tf_op jit(solution)/shard_map/tbd,de->tbe/dot_general | solution.py:53
  35.4 12.9 %all-gather = bf16[1,32,8,1536]{3,2,0,1:T(8,128)(2,1)S(1)} all-gather(bf16[1,16,8,1536]{3,2,0,1:T(8,128)(2,1)S(1)} %bitcast.270), channel_id=2, replica_groups=mesh['cfg'=2,'seq'=8,'mlp'=2] {'mlp'}, dimensions={1}, use_global_device_ids=true | all-gather | bytes 1179648 | tf_op jit(solution)/shard_map/all_gather | solution.py:118
  49.6 2.7 multiply_reduce_fusion.1
  57.7 2.6 fusion.61
  61.6 4.4 %copy.68 = bf16[768,1536]{1,0:T(8,128)(2,1)} copy(bf16[768,1536]{0,1:T(8,128)(2,1)} %get-tuple-element.178) | data formatting | bytes 4718592 | tf_op jit(solution)/shard_map/tbd,de->tbe/dot_general | solution.py:49
  66.0 4.3 %multiply_reduce_fusion.2 = (f32[32,8,12]{1,2,0:T(8,128)S(1)}, f32[32,8,12,64]{3,1,2,0:T(8,128)}) fusion(bf16[12,64,1536,1]{2,1,0,3:T(8,128)(2,1)} %bitcast.264, f32[8,1536]{1,0:T(8,128)S(1)} %copy-done.16, f32[8,1536]{1,0:T(8,128)S(1)} %copy-done.18, f32[32,8]{1,0:T(8,128)S(1)} %copy-done.20, f32[32,8]{1,0:T(8,128)S(1)} %broadcast_multiply_fusion.1, ...), kind=kOutput, calls=%fused_computation.77 | convolution fusion | flops 606729216 | bytes 4044800 | tf_op jit(solution)/shard_map/tbd,de->tbe/dot_general | solution.py:49
  73.8 25.3 %all-gather.7.cloned.1.call-done = bf16[8,154,1536]{2,1,0:T(8,128)(2,1)} async-done(((bf16[1,154,1536]{2,1,0:T(8,128)(2,1)}), bf16[8,154,1536]{2,1,0:T(8,128)(2,1)}) %all-gather.7.cloned.1.call-update) | async-done | bytes 3784720 | tf_op jit(solution)/shard_map/all_gather | solution.py:149
  99.1 7.8 %copy.73 = bf16[8,154,1536]{1,2,0:T(8,128)(2,1)} copy(bf16[8,154,1536]{2,1,0:T(8,128)(2,1)} %all-gather.7.cloned.1.call-done) | data formatting | bytes 7569408 | tf_op jit(solution)/shard_map/all_gather | solution.py:149
  106.9 6.5 %fusion.100 = (bf16[154,8,768]{0,2,1:T(8,128)(2,1)}, bf16[154,8,768]{0,2,1:T(8,128)(2,1)}) fusion(bf16[154,8,1536]{0,2,1:T(8,128)(2,1)} %bitcast.258), kind=kLoop, calls=%fused_computation.149 | loop fusion | bytes 7569408 | tf_op jit(solution)/shard_map/slice | solution.py:145
  114.8 26.2 %while.24 = (s32[]{:T(128)}, f32[8,12,32,64]{3,2,1,0:T(8,128)}, f32[8,12,32]{2,1,0:T(8,128)S(1)}, bf16[8,32,12,64]{3,1,2,0:T(8,128)(2,1)}, bf16[8,154,12,64]{1,3...) while((s32[]{:T(128)}, f32[8,12,32,64]{3,2,1,0:T(8,128)}, ...), condition=%wide.region_8.9_spmd, body=%wide.region_6.8_spmd.sunk | while | flops 15374978 | bytes 1339797 | solution.py:85
  116.1 1.9 fusion.120
  119.4 1.9 fusion.120
  129.3 1.9 fusion.120
  132.5 1.9 fusion.120
  135.8 1.9 fusion.120
  141.0 57.7 %all-gather.5.cloned.1.call-done = bf16[256,8,1536]{2,1,0:T(8,128)(2,1)} async-done(((bf16[32,8,1536]{2,1,0:T(8,128)(2,1)}), bf16[256,8,1536]{2,1,0:T(8,128)(2,1)}) %all-gather.5.cloned.1.call-update) | async-done | bytes 6291472 | tf_op jit(solution)/shard_map/all_gather | solution.py:148
  198.7 5.9 %fusion.99 = (bf16[256,8,768]{2,1,0:T(8,128)(2,1)}, bf16[256,8,768]{2,1,0:T(8,128)(2,1)}) fusion(bf16[256,8,1536]{2,1,0:T(8,128)(2,1)} %all-gather.5.cloned.1.call-done), kind=kLoop, calls=%fused_computation.148 | loop fusion | bytes 12582912 | tf_op jit(solution)/shard_map/slice | solution.py:145
  204.6 5.0 %copy.84 = bf16[256,8,768]{0,2,1:T(8,128)(2,1)} copy(bf16[256,8,768]{2,1,0:T(8,128)(2,1)} %get-tuple-element.180) | data formatting | bytes 6291456
  209.6 5.0 %copy.85 = bf16[256,8,768]{0,2,1:T(8,128)(2,1)} copy(bf16[256,8,768]{2,1,0:T(8,128)(2,1)} %get-tuple-element.179) | data formatting | bytes 6291456
  215.9 26.0 %while.25 = (s32[]{:T(128)}, f32[8,12,32,64]{3,2,1,0:T(8,128)}, f32[8,12,32]{2,1,0:T(8,128)S(1)}, bf16[8,32,12,64]{3,1,2,0:T(8,128)(2,1)}, bf16[8,256,12,64]{1,3...) while((s32[]{:T(128)}, f32[8,12,32,64]{3,2,1,0:T(8,128)}, f32[8,12,32]{2,1,0:T(8,128)S(1)}, ...), condition=%wide.region_12.13_spmd, body=%wide.region_10.12_spmd.sunk | while | flops 25460352 | bytes 1494609 | solution.py:85
  220.5 1.9 fusion.124
  223.8 1.9 fusion.124
  230.3 1.9 fusion.124
  241.9 2.4 fusion.79
  249.5 32.4 %all-reduce.2.cloned.1.call-done = bf16[32,8,1536]{2,1,0:T(8,128)(2,1)} async-done(((bf16[32,8,1536]{2,1,0:T(8,128)(2,1)}), bf16[32,8,1536]{2,1,0:T(8,128)(2,1)}) %all-reduce.2.cloned.1.call-update) | async-done | bytes 786448 | tf_op jit(solution)/shard_map/psum | solution.py:161
  284.3 7.0 %fusion.36 = bf16[32,8,3072]{2,1,0:T(8,128)(2,1)S(1)} fusion(bf16[1536,3072]{1,0:T(8,128)(2,1)} %param.27, f32[32,8,1536]{2,1,0:T(8,128)S(1)} %get-tuple-element.172, f32[8,1536]{1,0:T(8,128)S(1)} %copy-done.13, f32[8,1536]{1,0:T(8,128)S(1)} %copy-done.14, f32[32,8]{1,0:T(8,128)S(1)} %add_rsqrt_fusion.1, f32[32,8]{1,0:T(8,128)S(1)} %broadcast_multiply_fusion), kind=kOutput, calls=%fused_computation.42 | convolution fusion | flops 2424963072 | bytes 12683264 | tf_op jit(solution)/shard_map/tbd,du->tbu/dot_general | solution.py:169
  291.3 7.2 %fusion.39 = bf16[32,8,1536]{2,1,0:T(8,128)(2,1)} fusion(bf16[32,8,3072]{2,1,0:T(8,128)(2,1)S(1)} %fusion.36, bf16[3072,1536]{1,0:T(8,128)(2,1)} %param.28), kind=kOutput, calls=%fused_computation.43 | convolution fusion | flops 2416312320 | bytes 11796480 | tf_op jit(solution)/shard_map/tbu,ud->tbd/dot_general | solution.py:174
  298.6 17.6 %reduce-scatter.2.cloned.1.call-done = bf16[16,8,1536]{2,1,0:T(8,128)(2,1)} async-done(((bf16[32,8,1536]{2,1,0:T(8,128)(2,1)}), bf16[16,8,1536]{2,1,0:T(8,128)(2,1)}) %reduce-scatter.2.cloned.1.call-update) | async-done | bytes 393232 | tf_op jit(solution)/shard_map/reduce_scatter | solution.py:173
  (159 shorter events, 72.6 us)
Async XLA Ops:
  7.2 240.4 %copy-start = (bf16[768,1536]{1,0:T(8,128)(2,1)S(1)}, bf16[768,1536]{1,0:T(8,128)(2,1)}, u32[]{:S(2)}) copy-start(bf16[768,1536]{1,0:T(8,128)(2,1)} %param.24) | copy-start | bytes 7077892
  7.2 91.9 %all-gather.7.cloned.1.call-start = ((), (), s32[]{:S(2)}) async-start(), calls=%async_computation.4 | async-start | bytes 4423680 | tf_op jit(solution)/shard_map/all_gather | solution.py:149
  21.8 2.4 copy-start.4
  26.2 172.5 %all-gather.5.cloned.1.call-start = ((), (), s32[]{:S(2)}) async-start(), calls=%async_computation.1 | async-start | bytes 7077888 | tf_op jit(solution)/shard_map/all_gather | solution.py:148
  31.1 4.4 %copy-start.8 = (bf16[1,16,8,1536]{3,2,1,0:T(8,128)(2,1)S(1)}, bf16[1,16,8,1536]{3,2,1,0:T(8,128)(2,1)}, u32[]{:S(2)}) copy-start(bf16[1,16,8,1536]{3,2,1,0:T(8,128)(2,1)} %param.17) | copy-start | bytes 1179652
  35.4 13.4 %copy-start.6 = (f32[1,8,10,1536]{3,1,2,0:T(8,128)S(1)}, f32[1,8,10,1536]{3,1,2,0:T(8,128)}, u32[]{:S(2)}) copy-start(f32[1,8,10,1536]{3,1,2,0:T(8,128)} %param.19) | copy-start | bytes 1474564
  35.4 14.2 %copy-start.3 = (bf16[768,1536]{1,0:T(8,128)(2,1)S(1)}, bf16[768,1536]{1,0:T(8,128)(2,1)}, u32[]{:S(2)}) copy-start(bf16[768,1536]{1,0:T(8,128)(2,1)} %copy.75) | copy-start | bytes 7077892
  48.8 3.5 %copy-start.19 = (f32[32,8]{1,0:T(8,128)}, f32[32,8]{1,0:T(8,128)S(1)}, u32[]{:S(2)}) copy-start(f32[32,8]{1,0:T(8,128)S(1)} %add_rsqrt_fusion.3) | copy-start | bytes 3076
  49.6 2.7 copy-start.15
  49.6 2.7 copy-start.17
  49.6 3.1 copy-start.22
  61.3 220.6 %all-reduce.2.cloned.1.call-start = ((), (), s32[]{:S(2)}) async-start(), calls=%async_computation.2 | async-start | bytes 1572864 | tf_op jit(solution)/shard_map/psum | solution.py:161
  61.5 4.5 %copy-start.16 = (f32[8,1536]{1,0:T(8,128)S(1)}, f32[8,1536]{1,0:T(8,128)}, u32[]{:S(2)}) copy-start(f32[8,1536]{1,0:T(8,128)} %copy-done.15) | copy-start | bytes 147460
  61.6 4.5 %copy-start.18 = (f32[8,1536]{1,0:T(8,128)S(1)}, f32[8,1536]{1,0:T(8,128)}, u32[]{:S(2)}) copy-start(f32[8,1536]{1,0:T(8,128)} %copy-done.17) | copy-start | bytes 147460
  61.6 4.5 %copy-start.20 = (f32[32,8]{1,0:T(8,128)S(1)}, f32[32,8]{1,0:T(8,128)}, u32[]{:S(2)}) copy-start(f32[32,8]{1,0:T(8,128)} %copy-done.19) | copy-start | bytes 3076
  66.0 4.6 %copy-start.21 = (f32[64]{0:T(128)S(1)}, f32[64]{0:T(128)}, u32[]{:S(2)}) copy-start(f32[64]{0:T(128)} %get-tuple-element.192) | copy-start | bytes 772
  70.7 3.1 copy-start.23
  249.3 66.9 %reduce-scatter.2.cloned.1.call-start = ((), (), s32[]{:S(2)}) async-start(), calls=%async_computation.3 | async-start | bytes 1179648 | tf_op jit(solution)/shard_map/reduce_scatter | solution.py:173
  283.4 7.9 %copy-start.1 = (f32[32,8,1536]{2,1,0:T(8,128)}, f32[32,8,1536]{2,1,0:T(8,128)S(1)}, u32[]{:S(2)}) copy-start(f32[32,8,1536]{2,1,0:T(8,128)S(1)} %get-tuple-element.172) | copy-start | bytes 4718596
  283.4 0.8 copy-start.13
  283.4 0.9 copy-start.14
  291.3 24.9 %copy-start.7 = (f32[8,1536]{1,0:T(8,128)S(1)}, f32[8,1536]{1,0:T(8,128)}, u32[]{:S(2)}) copy-start(f32[8,1536]{1,0:T(8,128)} %get-tuple-element.183) | copy-start | bytes 147460
  298.5 20.7 %copy-start.11 = (f32[8,1536]{1,0:T(8,128)S(1)}, f32[8,1536]{1,0:T(8,128)}, u32[]{:S(2)}) copy-start(f32[8,1536]{1,0:T(8,128)} %get-tuple-element.184) | copy-start | bytes 147460
  298.6 20.7 %copy-start.12 = (f32[8,1536]{1,0:T(8,128)S(1)}, f32[8,1536]{1,0:T(8,128)}, u32[]{:S(2)}) copy-start(f32[8,1536]{1,0:T(8,128)} %get-tuple-element.185) | copy-start | bytes 147460
  298.6 20.7 %copy-start.24 = (bf16[1536,64]{0,1:T(8,128)(2,1)S(1)}, bf16[1536,64]{0,1:T(8,128)(2,1)}, u32[]{:S(2)}) copy-start(bf16[1536,64]{0,1:T(8,128)(2,1)} %param.29) | copy-start | bytes 589828
  316.2 3.1 copy-start.2
  316.2 3.1 copy-start.5
  317.8 3.2 copy-start.9
  319.7 1.3 collective-permute-start
  321.6 0.6 copy-start.10
Sparse Core Ops, SparseCore 0:
  26.3 72.7 all-gather.6
  101.3 97.3 all-gather.4
  249.4 32.4 all-reduce.1
  298.7 17.4 reduce-scatter.1
where the time goes:
time: 331 us; the launch traced here: 329 us
  waiting for transfers between devices  133 us (40%)
  matrix products  84.2 us (25%)
  local copies, waits for them, and re-layouts  64.4 us (19%)
  other arithmetic  18.2 us (5%)
  between operations  14.9 us (5%)
  blocking collectives  12.9 us (4%)
    all_gather x1, waiting for transfers between devices, shards(): lax.all_gather(own_pairs, 'seq', axis=0, tiled=True)  57.7 us
    psum x1, waiting for transfers between devices, shards(): lax.psum(jnp.einsum('tbe,ed->tbd', part, w_out, preferred_element_type=jn...  32.4 us
    dot_general x16, matrix products, one_prompt(): jnp.einsum('hqk,khd->hqd', weights.astype(jnp.bfloat16), values_one, pref...  30.6 us
    all_gather x1, waiting for transfers between devices, shards(): lax.all_gather(text_pairs, 'seq', axis=0, tiled=True)  25.3 us
    dot_general x16, matrix products, one_prompt(): jnp.einsum('qhd,khd->hqk', query_rows, keys_one, preferred_element_type=j...  21.4 us
    reduce_scatter x1, waiting for transfers between devices, shards(): lax.psum_scatter(jnp.einsum('tbu,ud->tbd', part, w_down, preferred_elemen...  17.6 us
    all_gather x1, blocking collectives, shards(): lax.all_gather(own_hidden, 'mlp', axis=0, tiled=True).astype(jnp.float32)  12.9 us
    slice x2, local copies, waits for them, and re-layouts, split_pairs(): pairs[..., width:].reshape(shape)  12.4 us
  transfers between devices with their start and end apart: 5, of which 5 were waited for; matrix products, arithmetic and copies ran while one was open for 23% of the time, Pallas kernels for 0%

commit v1 on v0

--- a/solution.py
+++ b/solution.py
@@ -10,6 +10,18 @@
 EPS = 1e-06
 GUIDE = 4.5
 SHIFT = 3.0
+
+
+def gather_around(value, axis, dim):
+    ways, here, turn = (lax.axis_size(axis), lax.axis_index(axis), value.shape[dim])
+    shape = [n * ways if d == dim else n for d, n in enumerate(value.shape)]
+    full = lax.dynamic_update_slice_in_dim(
+        jnp.zeros(shape, value.dtype), value, here * turn, axis=dim
+    )
+    for far in range(1, ways):
+        value = lax.ppermute(value, axis, [(d, (d + 1) % ways) for d in range(ways)])
+        full = lax.dynamic_update_slice_in_dim(full, value, (here - far) % ways * turn, axis=dim)
+    return full
 
 
 def partner_2(block, axis, stride):
@@ -145,7 +157,7 @@
         return (pairs[..., :width].reshape(shape), pairs[..., width:].reshape(shape))
 
     all_image, all_text = (
-        lax.all_gather(own_pairs, "seq", axis=0, tiled=True),
+        gather_around(own_pairs, "seq", 0),
         lax.all_gather(text_pairs, "seq", axis=0, tiled=True),
     )
     shaped = jnp.transpose(all_text.reshape(prompts, TXT, 2 * width), (1, 0, 2))

time: 331 us -> 642 us (1.94); the launches traced: 329 us -> 633 us
  local copies, waits for them, and re-layouts: 64.4 us -> 354 us
  waiting for transfers between devices: 133 us -> 146 us
    dynamic_update_slice x0 -> x8, local copies, waits for them, and re-layouts: none -> 266 us  [the longest x7 236 us: gather_around(): lax.dynamic_update_slice_in_dim(full, value, (here - far) % ways * turn,...]
    ppermute x0 -> x7, waiting for transfers between devices: none -> 93.1 us  [gather_around(): lax.ppermute(value, axis, [(d, (d + 1) % ways) for d in range(ways)])]
    all_gather x1 -> x0, waiting for transfers between devices: 57.7 us -> none  [shards(): lax.all_gather(own_pairs, 'seq', axis=0, tiled=True)]
    ppermute x0 -> x7, local copies, waits for them, and re-layouts: none -> 27.3 us  [gather_around(): lax.ppermute(value, axis, [(d, (d + 1) % ways) for d in range(ways)])]
    all_gather x1, waiting for transfers between devices: 25.3 us -> 0.01 us  [shards(): lax.all_gather(text_pairs, 'seq', axis=0, tiled=True)]
    unnamed x52 -> x60, local copies, waits for them, and re-layouts: 10.7 us -> 0.69 us
  transfers between devices with their start and end apart: 5 -> 11, of which waited for: 5 -> 9; matrix products, arithmetic and copies ran while one was open for 23% -> 57% of each run, Pallas kernels for 0% -> 0%
where the time goes in v1:
time: 642 us; the launch traced here: 633 us
  local copies, waits for them, and re-layouts  354 us (55%)
  waiting for transfers between devices  146 us (23%)
  matrix products  85.2 us (13%)
  other arithmetic  17.3 us (3%)
  between operations  14.9 us (2%)
  blocking collectives  13.1 us (2%)
    dynamic_update_slice x7, local copies, waits for them, and re-layouts, gather_around(): lax.dynamic_update_slice_in_dim(full, value, (here - far) % ways * turn,...  236 us
    ppermute x7, waiting for transfers between devices, gather_around(): lax.ppermute(value, axis, [(d, (d + 1) % ways) for d in range(ways)])  93.1 us
    psum x1, waiting for transfers between devices, shards(): lax.psum(jnp.einsum('tbe,ed->tbd', part, w_out, preferred_element_type=jn...  35 us
    dot_general x16, matrix products, one_prompt(): jnp.einsum('hqk,khd->hqd', weights.astype(jnp.bfloat16), values_one, pref...  30.7 us
    dynamic_update_slice x1, local copies, waits for them, and re-layouts, gather_around(): lax.dynamic_update_slice_in_dim(jnp.zeros(shape, value.dtype), value, her...  30.2 us
    ppermute x7, local copies, waits for them, and re-layouts, gather_around(): lax.ppermute(value, axis, [(d, (d + 1) % ways) for d in range(ways)])  27.3 us
    dot_general x16, matrix products, one_prompt(): jnp.einsum('qhd,khd->hqk', query_rows, keys_one, preferred_element_type=j...  21.4 us
    reduce_scatter x1, waiting for transfers between devices, shards(): lax.psum_scatter(jnp.einsum('tbu,ud->tbd', part, w_down, preferred_elemen...  17.6 us
  transfers between devices with their start and end apart: 11, of which 9 were waited for; matrix products, arithmetic and copies ran while one was open for 57% of the time, Pallas kernels for 0%

profile of v1, /device:TPU:0, one launch (start us, length us, event | category | flops | bytes accessed | tf_op | source)
XLA Modules:
  0.0 633.3 jit_solution(16348302127439707476)
XLA Ops:
  7.2 13.1 %all-gather = bf16[1,32,8,1536]{3,2,0,1:T(8,128)(2,1)S(1)} all-gather(bf16[1,16,8,1536]{3,2,0,1:T(8,128)(2,1)} %bitcast.270), channel_id=2, replica_groups=mesh['cfg'=2,'seq'=8,'mlp'=2] {'mlp'}, dimensions={1}, use_global_device_ids=true | all-gather | bytes 1179648 | tf_op jit(solution)/shard_map/all_gather | solution.py:130
  21.6 4.9 slice_bitcast_fusion
  26.5 4.3 copy.99
  45.7 19.7 %collective-permute-done = bf16[32,8,1536]{2,1,0:T(8,128)(2,1)S(1)} collective-permute-done((bf16[32,8,1536]{2,1,0:T(8,128)(2,1)S(1)}, bf16[32,8,1536]{2,1,0:T(8,128)(2,1)S(1)}, u32[]{:S(2)}, u32[]{:S(2)}) %collective-permute-start) | collective-permute-done | bytes 786464 | tf_op jit(solution)/shard_map/ppermute | solution.py:22
  65.6 20.4 %collective-permute-done.1 = bf16[32,8,1536]{2,1,0:T(8,128)(2,1)} collective-permute-done((bf16[32,8,1536]{2,1,0:T(8,128)(2,1)S(1)}, bf16[32,8,1536]{2,1,0:T(8,128)(2,1)}, u32[]{:S(2)}, u32[]{:S(2)}) %collective-permute-start.1) | collective-permute-done | bytes 786464 | tf_op jit(solution)/shard_map/ppermute | solution.py:22
  90.6 15.3 %collective-permute-done.2 = bf16[32,8,1536]{2,1,0:T(8,128)(2,1)} collective-permute-done((bf16[32,8,1536]{2,1,0:T(8,128)(2,1)}, bf16[32,8,1536]{2,1,0:T(8,128)(2,1)}, u32[]{:S(2)}, u32[]{:S(2)}) %collective-permute-start.2) | collective-permute-done | bytes 786464 | tf_op jit(solution)/shard_map/ppermute | solution.py:22
  105.9 4.3 copy.95
  113.5 11.3 %collective-permute-done.3 = bf16[32,8,1536]{2,1,0:T(8,128)(2,1)} collective-permute-done((bf16[32,8,1536]{2,1,0:T(8,128)(2,1)}, bf16[32,8,1536]{2,1,0:T(8,128)(2,1)}, u32[]{:S(2)}, u32[]{:S(2)}) %collective-permute-start.3) | collective-permute-done | bytes 786464 | tf_op jit(solution)/shard_map/ppermute | solution.py:22
  126.7 16.1 %collective-permute-done.4 = bf16[32,8,1536]{2,1,0:T(8,128)(2,1)} collective-permute-done((bf16[32,8,1536]{2,1,0:T(8,128)(2,1)}, bf16[32,8,1536]{2,1,0:T(8,128)(2,1)}, u32[]{:S(2)}, u32[]{:S(2)}) %collective-permute-start.4) | collective-permute-done | bytes 786464 | tf_op jit(solution)/shard_map/ppermute | solution.py:22
  146.1 4.3 copy.92
  150.4 10.3 %collective-permute-done.5 = bf16[32,8,1536]{2,1,0:T(8,128)(2,1)} collective-permute-done((bf16[32,8,1536]{2,1,0:T(8,128)(2,1)}, bf16[32,8,1536]{2,1,0:T(8,128)(2,1)}, u32[]{:S(2)}, u32[]{:S(2)}) %collective-permute-start.5) | collective-permute-done | bytes 786464 | tf_op jit(solution)/shard_map/ppermute | solution.py:22
  160.7 4.3 multiply_reduce_fusion.2
  165.0 3.9 copy.103
  175.5 30.2 %dynamic_update_slice.38 = bf16[256,8,1536]{0,2,1:T(8,128)(2,1)} dynamic-update-slice(bf16[256,8,1536]{0,2,1:T(8,128)(2,1)} %broadcast_in_dim.15, bf16[32,8,1536]{0,2,1:T(8,128)(2,1)} %copy.103, s32[]{:T(128)S(6)} %select_n.87, s32[]{:T(128)} %constant.153.clone.1, s32[]{:T(128)} %constant.153.clone.1) | dynamic-update-slice | bytes 1572868 | tf_op jit(solution)/shard_map/dynamic_update_slice | solution.py:18
  205.7 3.9 copy.104
  209.6 34.0 %dynamic_update_slice.39 = bf16[256,8,1536]{0,2,1:T(8,128)(2,1)} dynamic-update-slice(bf16[256,8,1536]{0,2,1:T(8,128)(2,1)} %dynamic_update_slice.38, bf16[32,8,1536]{0,2,1:T(8,128)(2,1)} %copy.104, s32[]{:T(128)S(6)} %select_n.89, s32[]{:T(128)} %constant.153.clone.1, s32[]{:T(128)} %constant.153.clone.1) | dynamic-update-slice | bytes 1572868 | tf_op jit(solution)/shard_map/dynamic_update_slice | solution.py:23
  247.5 34.0 %dynamic_update_slice.40 = bf16[256,8,1536]{0,2,1:T(8,128)(2,1)} dynamic-update-slice(bf16[256,8,1536]{0,2,1:T(8,128)(2,1)} %dynamic_update_slice.39, bf16[32,8,1536]{0,2,1:T(8,128)(2,1)} %copy.105, s32[]{:T(128)S(6)} %select_n.91, s32[]{:T(128)} %constant.153.clone.1, s32[]{:T(128)} %constant.153.clone.1) | dynamic-update-slice | bytes 1572868 | tf_op jit(solution)/shard_map/dynamic_update_slice | solution.py:23
  285.4 34.0 %dynamic_update_slice.41 = bf16[256,8,1536]{0,2,1:T(8,128)(2,1)} dynamic-update-slice(bf16[256,8,1536]{0,2,1:T(8,128)(2,1)} %dynamic_update_slice.40, bf16[32,8,1536]{0,2,1:T(8,128)(2,1)} %copy.106, s32[]{:T(128)S(6)} %select_n.93, s32[]{:T(128)} %constant.153.clone.1, s32[]{:T(128)} %constant.153.clone.1) | dynamic-update-slice | bytes 1572868 | tf_op jit(solution)/shard_map/dynamic_update_slice | solution.py:23
  323.4 28.9 %dynamic_update_slice.42 = bf16[256,8,1536]{0,2,1:T(8,128)(2,1)} dynamic-update-slice(bf16[256,8,1536]{0,2,1:T(8,128)(2,1)} %dynamic_update_slice.41, bf16[32,8,1536]{0,2,1:T(8,128)(2,1)} %copy.107, s32[]{:T(128)S(6)} %select_n.95, s32[]{:T(128)} %constant.153.clone.1, s32[]{:T(128)} %constant.153.clone.1) | dynamic-update-slice | bytes 1572868 | tf_op jit(solution)/shard_map/dynamic_update_slice | solution.py:23
  356.2 35.0 %dynamic_update_slice.43 = bf16[256,8,1536]{0,2,1:T(8,128)(2,1)} dynamic-update-slice(bf16[256,8,1536]{0,2,1:T(8,128)(2,1)} %dynamic_update_slice.42, bf16[32,8,1536]{0,2,1:T(8,128)(2,1)} %copy.108, s32[]{:T(128)S(6)} %select_n.97, s32[]{:T(128)} %constant.153.clone.1, s32[]{:T(128)} %constant.153.clone.1) | dynamic-update-slice | bytes 1572868 | tf_op jit(solution)/shard_map/dynamic_update_slice | solution.py:23
  395.1 35.0 %dynamic_update_slice.44 = bf16[256,8,1536]{0,2,1:T(8,128)(2,1)} dynamic-update-slice(bf16[256,8,1536]{0,2,1:T(8,128)(2,1)} %dynamic_update_slice.43, bf16[32,8,1536]{0,2,1:T(8,128)(2,1)} %copy.109, s32[]{:T(128)S(6)} %select_n.99, s32[]{:T(128)} %constant.153.clone.1, s32[]{:T(128)} %constant.153.clone.1) | dynamic-update-slice | bytes 1572868 | tf_op jit(solution)/shard_map/dynamic_update_slice | solution.py:23
  430.1 3.9 copy.110
  434.0 35.0 %dynamic_update_slice.45 = bf16[256,8,1536]{0,2,1:T(8,128)(2,1)} dynamic-update-slice(bf16[256,8,1536]{0,2,1:T(8,128)(2,1)} %dynamic_update_slice.44, bf16[32,8,1536]{0,2,1:T(8,128)(2,1)} %copy.110, s32[]{:T(128)S(6)} %select_n.101, s32[]{:T(128)} %constant.153.clone.1, s32[]{:T(128)} %constant.153.clone.1) | dynamic-update-slice | bytes 1572868 | tf_op jit(solution)/shard_map/dynamic_update_slice | solution.py:23
  468.9 6.0 fusion.99
  476.3 26.1 %while.25 = (s32[]{:T(128)}, f32[8,12,32,64]{3,2,1,0:T(8,128)}, f32[8,12,32]{2,1,0:T(8,128)S(1)}, bf16[8,32,12,64]{3,1,2,0:T(8,128)(2,1)}, bf16[8,256,12,64]{1,3...) while((s32[]{:T(128)}, f32[8,12,32,64]{3,2,1,0:T(8,128)}, f32[8,12,32]{2,1,0:T(8,128)S(1)}, ...), condition=%wide.region_12.13_spmd, body=%wide.region_10.12_spmd.sunk | while | flops 25460352 | bytes 1494609 | solution.py:97
  502.4 7.7 %copy.97 = bf16[8,154,1536]{1,2,0:T(8,128)(2,1)} copy(bf16[8,154,1536]{2,1,0:T(8,128)(2,1)} %all-gather.4.cloned.1.call-done) | data formatting | bytes 7569408 | tf_op jit(solution)/shard_map/all_gather | solution.py:161
  510.1 6.0 fusion.100
  517.5 26.2 %while.24 = (s32[]{:T(128)}, f32[8,12,32,64]{3,2,1,0:T(8,128)}, f32[8,12,32]{2,1,0:T(8,128)S(1)}, bf16[8,32,12,64]{3,1,2,0:T(8,128)(2,1)}, bf16[8,154,12,64]{1,3...) while((s32[]{:T(128)}, f32[8,12,32,64]{3,2,1,0:T(8,128)}, ...), condition=%wide.region_8.9_spmd, body=%wide.region_6.8_spmd.sunk | while | flops 15374978 | bytes 1339797 | solution.py:97
  551.4 35.0 %all-reduce.2.cloned.1.call-done = bf16[32,8,1536]{2,1,0:T(8,128)(2,1)} async-done(((bf16[32,8,1536]{2,1,0:T(8,128)(2,1)}), bf16[32,8,1536]{2,1,0:T(8,128)(2,1)}) %all-reduce.2.cloned.1.call-update) | async-done | bytes 786448 | tf_op jit(solution)/shard_map/psum | solution.py:173
  588.8 7.0 %fusion.36 = bf16[32,8,3072]{2,1,0:T(8,128)(2,1)S(1)} fusion(bf16[1536,3072]{1,0:T(8,128)(2,1)} %param.27, f32[32,8,1536]{2,1,0:T(8,128)S(1)} %get-tuple-element.172, f32[8,1536]{1,0:T(8,128)S(1)} %copy-done.17, f32[8,1536]{1,0:T(8,128)S(1)} %copy-done.18, f32[32,8]{1,0:T(8,128)S(1)} %add_rsqrt_fusion.1, f32[32,8]{1,0:T(8,128)S(1)} %broadcast_multiply_fusion), kind=kOutput, calls=%fused_computation.42 | convolution fusion | flops 2424963072 | bytes 12683264 | tf_op jit(solution)/shard_map/tbd,du->tbu/dot_general | solution.py:181
  595.8 7.2 %fusion.39 = bf16[32,8,1536]{2,1,0:T(8,128)(2,1)} fusion(bf16[32,8,3072]{2,1,0:T(8,128)(2,1)S(1)} %fusion.36, bf16[3072,1536]{1,0:T(8,128)(2,1)} %param.28), kind=kOutput, calls=%fused_computation.43 | convolution fusion | flops 2416312320 | bytes 11796480 | tf_op jit(solution)/shard_map/tbu,ud->tbd/dot_general | solution.py:186
  603.1 17.6 %reduce-scatter.2.cloned.1.call-done = bf16[16,8,1536]{2,1,0:T(8,128)(2,1)} async-done(((bf16[32,8,1536]{2,1,0:T(8,128)(2,1)}), bf16[16,8,1536]{2,1,0:T(8,128)(2,1)}) %reduce-scatter.2.cloned.1.call-update) | async-done | bytes 393232 | tf_op jit(solution)/shard_map/reduce_scatter | solution.py:185
  (195 shorter events, 125.5 us)
Async XLA Ops:
  7.2 542.4 %copy-start = (bf16[768,1536]{1,0:T(8,128)(2,1)S(1)}, bf16[768,1536]{1,0:T(8,128)(2,1)}, u32[]{:S(2)}) copy-start(bf16[768,1536]{1,0:T(8,128)(2,1)} %param.24) | copy-start | bytes 7077892
  7.2 495.2 %all-gather.4.cloned.1.call-start = ((), (), s32[]{:S(2)}) async-start(), calls=%async_computation.3 | async-start | bytes 4423680 | tf_op jit(solution)/shard_map/all_gather | solution.py:161
  7.2 13.7 %copy-start.10 = (f32[1,8,10,1536]{3,1,2,0:T(8,128)S(1)}, f32[1,8,10,1536]{3,1,2,0:T(8,128)}, u32[]{:S(2)}) copy-start(f32[1,8,10,1536]{3,1,2,0:T(8,128)} %param.19) | copy-start | bytes 1474564
  20.9 13.3 %copy-start.23 = (f32[32,8]{1,0:T(8,128)}, f32[32,8]{1,0:T(8,128)S(1)}, u32[]{:S(2)}) copy-start(f32[32,8]{1,0:T(8,128)S(1)} %add_rsqrt_fusion.3) | copy-start | bytes 3076
  21.6 12.6 %copy-start.19 = (f32[8,1536]{1,0:T(8,128)}, f32[8,1536]{1,0:T(8,128)S(1)}, u32[]{:S(2)}) copy-start(f32[8,1536]{1,0:T(8,128)S(1)} %get-tuple-element.188) | copy-start | bytes 147460
  21.6 12.6 %copy-start.21 = (f32[8,1536]{1,0:T(8,128)}, f32[8,1536]{1,0:T(8,128)S(1)}, u32[]{:S(2)}) copy-start(f32[8,1536]{1,0:T(8,128)S(1)} %get-tuple-element.189) | copy-start | bytes 147460
  42.8 22.7 %copy-start.3 = (bf16[1,154,1536]{2,1,0:T(8,128)(2,1)S(1)}, bf16[1,154,1536]{2,1,0:T(8,128)(2,1)}, u32[]{:S(2)}) copy-start(bf16[1,154,1536]{2,1,0:T(8,128)(2,1)} %param.18) | copy-start | bytes 1419268
  43.9 21.7 %copy-start.4 = (bf16[32,8,1536]{2,1,0:T(8,128)(2,1)}, bf16[32,8,1536]{2,1,0:T(8,128)(2,1)S(1)}, u32[]{:S(2)}) copy-start(bf16[32,8,1536]{2,1,0:T(8,128)(2,1)S(1)} %pad_maximum_fusion) | copy-start | bytes 2359300
  43.9 21.5 %collective-permute-start = (bf16[32,8,1536]{2,1,0:T(8,128)(2,1)S(1)}, bf16[32,8,1536]{2,1,0:T(8,128)(2,1)S(1)}, u32[]{:S(2)}, u32[]{:S(2)}) collective-permute-start(bf16[32,8,1536]{2,1,0:T(8,128)(2,1)S(1)} %pad_maximum_fusion), channel_id=1, source_target_pairs={{0,2},{2,4},{4,6},{6,8},{8,10},{10,12},{12,14},{14,0},{1,3},{3,5},... | collective-permute-start | bytes 2359304 | tf_op jit(solution)/shard_map/ppermute | solution.py:22
  65.4 20.6 %copy-start.9 = (bf16[32,8,1536]{2,1,0:T(8,128)(2,1)}, bf16[32,8,1536]{2,1,0:T(8,128)(2,1)S(1)}, u32[]{:S(2)}) copy-start(bf16[32,8,1536]{2,1,0:T(8,128)(2,1)S(1)} %collective-permute-done) | copy-start | bytes 2359300
  65.4 20.6 %collective-permute-start.1 = (bf16[32,8,1536]{2,1,0:T(8,128)(2,1)S(1)}, bf16[32,8,1536]{2,1,0:T(8,128)(2,1)}, u32[]{:S(2)}, u32[]{:S(2)}) collective-permute-start(bf16[32,8,1536]{2,1,0:T(8,128)(2,1)S(1)} %collective-permute-done), channel_id=1, source_target_pairs={{0,2},{2,4},{4,6},{6,8},{8,10},{10,12},{12,14},{14,0},{1,3},{3,5},... | collective-permute-start | bytes 2359304 | tf_op jit(solution)/shard_map/ppermute | solution.py:22
  86.0 19.9 %collective-permute-start.2 = (bf16[32,8,1536]{2,1,0:T(8,128)(2,1)}, bf16[32,8,1536]{2,1,0:T(8,128)(2,1)}, u32[]{:S(2)}, u32[]{:S(2)}) collective-permute-start(bf16[32,8,1536]{2,1,0:T(8,128)(2,1)} %collective-permute-done.1), channel_id=1, source_target_pairs={{0,2},{2,4},{4,6},{6,8},{8,10},{10,12},{12,14},{14,0},{1,3},{3,5},... | collective-permute-start | bytes 2359304 | tf_op jit(solution)/shard_map/ppermute | solution.py:22
  105.8 18.9 %collective-permute-start.3 = (bf16[32,8,1536]{2,1,0:T(8,128)(2,1)}, bf16[32,8,1536]{2,1,0:T(8,128)(2,1)}, u32[]{:S(2)}, u32[]{:S(2)}) collective-permute-start(bf16[32,8,1536]{2,1,0:T(8,128)(2,1)} %collective-permute-done.2), channel_id=1, source_target_pairs={{0,2},{2,4},{4,6},{6,8},{8,10},{10,12},{12,14},{14,0},{1,3},{3,5},... | collective-permute-start | bytes 2359304 | tf_op jit(solution)/shard_map/ppermute | solution.py:22
  110.1 14.6 %copy-start.5 = (bf16[768,1536]{1,0:T(8,128)(2,1)S(1)}, bf16[768,1536]{1,0:T(8,128)(2,1)}, u32[]{:S(2)}) copy-start(bf16[768,1536]{1,0:T(8,128)(2,1)} %copy.95) | copy-start | bytes 7077892
  113.5 12.1 %copy-start.11 = (bf16[154,1536]{1,0:T(8,128)(2,1)}, bf16[154,1536]{1,0:T(8,128)(2,1)S(1)}, u32[]{:S(2)}) copy-start(bf16[154,1536]{1,0:T(8,128)(2,1)S(1)} %fusion.43) | copy-start | bytes 1419268
  124.8 18.0 %collective-permute-start.4 = (bf16[32,8,1536]{2,1,0:T(8,128)(2,1)}, bf16[32,8,1536]{2,1,0:T(8,128)(2,1)}, u32[]{:S(2)}, u32[]{:S(2)}) collective-permute-start(bf16[32,8,1536]{2,1,0:T(8,128)(2,1)} %collective-permute-done.3), channel_id=1, source_target_pairs={{0,2},{2,4},{4,6},{6,8},{8,10},{10,12},{12,14},{14,0},{1,3},{3,5},... | collective-permute-start | bytes 2359304 | tf_op jit(solution)/shard_map/ppermute | solution.py:22
  126.7 18.5 %copy-start.8 = (bf16[154,768]{1,0:T(8,128)(2,1)S(1)}, bf16[154,768]{1,0:T(8,128)(2,1)}, u32[]{:S(2)}) copy-start(bf16[154,768]{1,0:T(8,128)(2,1)} %copy.96) | copy-start | bytes 709636
  142.8 17.9 %collective-permute-start.5 = (bf16[32,8,1536]{2,1,0:T(8,128)(2,1)}, bf16[32,8,1536]{2,1,0:T(8,128)(2,1)}, u32[]{:S(2)}, u32[]{:S(2)}) collective-permute-start(bf16[32,8,1536]{2,1,0:T(8,128)(2,1)} %collective-permute-done.4), channel_id=1, source_target_pairs={{0,2},{2,4},{4,6},{6,8},{8,10},{10,12},{12,14},{14,0},{1,3},{3,5},... | collective-permute-start | bytes 2359304 | tf_op jit(solution)/shard_map/ppermute | solution.py:22
  146.0 440.4 %all-reduce.2.cloned.1.call-start = ((), (), s32[]{:S(2)}) async-start(), calls=%async_computation.1 | async-start | bytes 1572864 | tf_op jit(solution)/shard_map/psum | solution.py:173
  146.1 14.6 %copy-start.20 = (f32[8,1536]{1,0:T(8,128)S(1)}, f32[8,1536]{1,0:T(8,128)}, u32[]{:S(2)}) copy-start(f32[8,1536]{1,0:T(8,128)} %copy-done.19) | copy-start | bytes 147460
  146.1 14.6 %copy-start.22 = (f32[8,1536]{1,0:T(8,128)S(1)}, f32[8,1536]{1,0:T(8,128)}, u32[]{:S(2)}) copy-start(f32[8,1536]{1,0:T(8,128)} %copy-done.21) | copy-start | bytes 147460
  146.1 14.6 %copy-start.24 = (f32[32,8]{1,0:T(8,128)S(1)}, f32[32,8]{1,0:T(8,128)}, u32[]{:S(2)}) copy-start(f32[32,8]{1,0:T(8,128)} %copy-done.23) | copy-start | bytes 3076
  160.7 269.4 %collective-permute-start.6 = (bf16[32,8,1536]{2,1,0:T(8,128)(2,1)}, bf16[32,8,1536]{2,1,0:T(8,128)(2,1)}, u32[]{:S(2)}, u32[]{:S(2)}) collective-permute-start(bf16[32,8,1536]{2,1,0:T(8,128)(2,1)} %collective-permute-done.5), channel_id=1, source_target_pairs={{0,2},{2,4},{4,6},{6,8},{8,10},{10,12},{12,14},{14,0},{1,3},{3,5},... | collective-permute-start | bytes 2359304 | tf_op jit(solution)/shard_map/ppermute | solution.py:22
  165.0 4.2 copy-start.26
  175.5 30.2 %copy-start.28 = (s32[1,8]{1,0:T(1,128)S(1)}, s32[1,8]{1,0:T(1,128)}, u32[]{:S(2)}) copy-start(s32[1,8]{1,0:T(1,128)} %param.20) | copy-start | bytes 100
  551.3 69.4 %reduce-scatter.2.cloned.1.call-start = ((), (), s32[]{:S(2)}) async-start(), calls=%async_computation.2 | async-start | bytes 1179648 | tf_op jit(solution)/shard_map/reduce_scatter | solution.py:185
  587.9 7.9 %copy-start.1 = (f32[32,8,1536]{2,1,0:T(8,128)}, f32[32,8,1536]{2,1,0:T(8,128)S(1)}, u32[]{:S(2)}) copy-start(f32[32,8,1536]{2,1,0:T(8,128)S(1)} %get-tuple-element.172) | copy-start | bytes 4718596
  595.8 24.9 %copy-start.12 = (f32[8,1536]{1,0:T(8,128)S(1)}, f32[8,1536]{1,0:T(8,128)}, u32[]{:S(2)}) copy-start(f32[8,1536]{1,0:T(8,128)} %get-tuple-element.183) | copy-start | bytes 147460
  603.0 20.7 %copy-start.15 = (f32[8,1536]{1,0:T(8,128)S(1)}, f32[8,1536]{1,0:T(8,128)}, u32[]{:S(2)}) copy-start(f32[8,1536]{1,0:T(8,128)} %get-tuple-element.184) | copy-start | bytes 147460
  603.1 20.7 %copy-start.16 = (f32[8,1536]{1,0:T(8,128)S(1)}, f32[8,1536]{1,0:T(8,128)}, u32[]{:S(2)}) copy-start(f32[8,1536]{1,0:T(8,128)} %get-tuple-element.185) | copy-start | bytes 147460
  603.1 20.7 %copy-start.29 = (bf16[1536,64]{0,1:T(8,128)(2,1)S(1)}, bf16[1536,64]{0,1:T(8,128)(2,1)}, u32[]{:S(2)}) copy-start(bf16[1536,64]{0,1:T(8,128)(2,1)} %param.29) | copy-start | bytes 589828
  624.2 1.3 collective-permute-start.7
  (9 other events, 19.1 us)
Sparse Core Ops, SparseCore 0:
  146.1 83.6 all-gather.3
  551.4 34.9 all-reduce.1
  603.2 17.4 reduce-scatter.1
